TPU v7x, 256 devices: a whole 4x4x8 slice. The times are simulated.
256 devices in a mesh: prompt: 4 (over x), vocab: 64 (over z, y, core).
Axes of the slice: x: 4, y: 4, z: 8, core: 2. Of those that a mesh axis runs over, the one named last changes fastest.
Arguments:
- hidden: bfloat16 [512, 8192], P('prompt')
- head: bfloat16 [8192, 65536], P('prompt', 'vocab')
- gain: float32 [8192], replicated, may hold values from 0.25 to 1.75
- refusal_ids: int32 [512, 16], P('prompt'), may hold values from 0 to 65535, as said below
- refusal_count: int32 [512], P('prompt'), may hold values from 1 to 16
- loss_scale: float32 [512], P('prompt'), may hold values from 8 to 32
Outputs:
- grad_hidden: float32 [512, 8192], P('prompt', 'vocab')
- log_refusal: float32 [512], P('prompt')
Inputs may be any that keep to these rules, and one draw needn't show every extreme that they name: `refusal_ids`: the first refusal_count entries of a prompt's list are distinct ids below 65536; later entries are ignored.
All inputs are finite; a program needn't handle non-finite values.
Results may differ from a plain program's by a relative error of at most 0.0027.
The roundings to bfloat16 on the way count: a program that leaves them out, or rounds other values in their place, can miss the bound.
Values may be sent and summed in bfloat16 or wider, within the bound.
A program may use at most 128 MiB of HBM per device.

v0:
```python
import jax
import jax.numpy as jnp
from jax import lax
from jax.sharding import PartitionSpec as P

epsilon = 1e-05
lowest = -1e30


def shards(hidden, head, gain, refusal_ids, refusal_count, loss_scale):
    row_count, model_width = hidden.shape
    vocab_local = head.shape[1]
    list_length = refusal_ids.shape[1]
    hidden_f = hidden.astype(jnp.float32)
    inverse_rms = lax.rsqrt(jnp.mean(hidden_f * hidden_f, axis=1, keepdims=True) + epsilon)
    normed = (hidden_f * inverse_rms * gain).astype(jnp.bfloat16)
    logits = jnp.dot(
        normed,
        lax.all_gather(head, "prompt", axis=0, tiled=True),
        preferred_element_type=jnp.float32,
    )
    vocab_start = lax.axis_index("vocab") * vocab_local
    shifted_ids = refusal_ids - vocab_start
    in_list = jnp.arange(list_length)[None, :] < refusal_count[:, None]
    is_local = in_list & (shifted_ids >= 0) & (shifted_ids < vocab_local)
    safe_ids = jnp.clip(shifted_ids, 0, vocab_local - 1)
    picked = jnp.take_along_axis(logits, safe_ids, axis=1)
    peak_all = jnp.max(logits, axis=1)
    peak_ref = jnp.max(jnp.where(is_local, picked, lowest), axis=1)
    peak_all, peak_ref = lax.pmax((peak_all, peak_ref), "vocab")
    sum_all = jnp.sum(jnp.exp(logits - peak_all[:, None]), axis=1)
    sum_ref = jnp.sum(jnp.exp(jnp.where(is_local, picked - peak_ref[:, None], lowest)), axis=1)
    sum_all, sum_ref = lax.psum((sum_all, sum_ref), "vocab")
    lse_all = peak_all + jnp.log(sum_all)
    lse_ref = peak_ref + jnp.log(sum_ref)
    log_refusal = lse_ref - lse_all
    member = jnp.any(
        (safe_ids[:, :, None] == jnp.arange(vocab_local)[None, None, :]) & is_local[:, :, None],
        axis=1,
    )
    grad_logits = loss_scale[:, None] * (
        jnp.exp(jnp.where(member, logits - lse_ref[:, None], lowest))
        - jnp.exp(logits - lse_all[:, None])
    )
    grad_b = grad_logits.astype(jnp.bfloat16)
    slice_width = model_width // lax.axis_size("vocab")
    col_start = lax.axis_index("vocab") * slice_width
    grad_full = lax.dot_general(
        grad_b,
        lax.all_gather(head, "prompt", axis=0, tiled=True),
        (((1,), (1,)), ((), ())),
        preferred_element_type=jnp.float32,
    )
    grad_cols = lax.psum_scatter(grad_full, "vocab", scatter_dimension=1, tiled=True)
    normed_cols = lax.dynamic_slice_in_dim(normed, col_start, slice_width, 1).astype(jnp.float32)
    row_term = lax.psum(jnp.sum(grad_cols * normed_cols, axis=1), "vocab")
    hidden_cols = lax.dynamic_slice_in_dim(hidden_f, col_start, slice_width, 1)
    gain_cols = lax.dynamic_slice_in_dim(gain, col_start, slice_width, 0)
    grad_hidden = (
        inverse_rms * gain_cols * grad_cols
        - hidden_cols * (inverse_rms * inverse_rms / model_width) * row_term[:, None]
    )
    return (grad_hidden, log_refusal)


def solution(mesh):
    return jax.shard_map(
        shards,
        mesh=mesh,
        in_specs=(
            P("prompt", None),
            P("prompt", "vocab"),
            P(),
            P("prompt", None),
            P("prompt"),
            P("prompt"),
        ),
        out_specs=(P("prompt", "vocab"), P("prompt")),
        check_vma=False,
    )
```

profile of v0, /device:TPU:1, one launch (start us, length us, event | category | flops | bytes accessed | tf_op | source)
XLA Modules:
  0.0 739.2 jit_solution(6245504685200072266)
XLA Ops:
  7.2 0.0 copy-start.2
  7.2 0.0 copy-start
  7.2 0.0 copy-start.1
  7.2 0.0 all-gather.2.cloned.1.call-start
  7.2 0.7 all-gather.2.cloned.1.call-update
  7.9 0.0 reduce-scatter.2.cloned.1.call-start
  8.0 0.1 copy.11
  8.1 0.1 reshape.39
  8.2 0.6 copy-done
  8.8 0.5 multiply_reduce_fusion
  9.3 1.9 multiply_convert_fusion
  11.2 159.1 %all-gather.2.cloned.1.call-done = bf16[8192,1024]{1,0:T(8,128)(2,1)} async-done(((bf16[2048,1024]{1,0:T(8,128)(2,1)}), bf16[8192,1024]{1,0:T(8,128)(2,1)}) %all-gather.2.cloned.1.call-update) | async-done | bytes 16777232 | tf_op jit(solution)/shard_map/all_gather | solution.py:19
  170.3 8.8 %fusion.12 = (f32[128]{0:T(128)S(1)}, f32[128,1024]{1,0:T(8,128)S(1)}) fusion(bf16[128,8192]{1,0:T(8,128)(2,1)} %multiply_convert_fusion, bf16[8192,1024]{1,0:T(8,128)(2,1)} %all-gather.2.cloned.1.call-done), kind=kOutput, calls=%fused_computation.30 | convolution fusion | flops 2147614720 | bytes 19399168 | tf_op jit(solution)/shard_map/dot_general | solution.py:17
  179.1 0.0 copy-start.4
  179.1 0.0 copy-start.3
  179.2 16.6 %gather_fusion = f32[2048]{0:T(1024)S(1)} fusion(f32[128,1024]{1,0:T(8,128)S(1)} %get-tuple-element.16, s32[2048]{0:T(1024)S(1)} %reshape.39), kind=kCustom, calls=%fused_computation | custom fusion | bytes 32768 | tf_op jit(solution)/shard_map/jit(take_along_axis)/gather | solution.py:27
  195.8 0.1 reshape.42
  195.9 0.2 select_reduce_fusion
  196.1 2.4 fusion.1
  198.5 124.6 %all-reduce.1 = (f32[128]{0:T(128)S(1)}, f32[128]{0:T(128)S(1)}) all-reduce(f32[128]{0:T(128)S(1)} %get-tuple-element.15, f32[128]{0:T(128)S(1)} %get-tuple-element.9), channel_id=1, replica_groups=mesh['prompt'=4,'vocab'=64] {'vocab'}, use_global_device_ids=true, to_apply=%region_7.8 | all-reduce | flops 256 | bytes 2048 | tf_op jit(solution)/shard_map/pmax | solution.py:30
  323.1 0.2 exponential_reduce_fusion.1
  323.3 0.2 exponential_reduce_fusion
  323.5 128.4 %all-reduce = (f32[128]{0:T(128)S(1)}, f32[128]{0:T(128)S(1)}) all-reduce(f32[128]{0:T(128)S(1)} %exponential_reduce_fusion, f32[128]{0:T(128)S(1)} %exponential_reduce_fusion.1), channel_id=1, replica_groups=mesh['prompt'=4,'vocab'=64] {'vocab'}, use_global_device_ids=true, to_apply=%region_9.10 | all-reduce | flops 256 | bytes 2048 | tf_op jit(solution)/shard_map/psum | solution.py:33
  452.0 0.5 fusion.10
  452.5 13.4 %fusion.2 = f32[128,8192]{1,0:T(8,128)} fusion(bf16[8192,1024]{1,0:T(8,128)(2,1)} %all-gather.2.cloned.1.call-done, f32[128,1024]{1,0:T(8,128)S(1)} %get-tuple-element.16, pred[128,1024]{1,0:T(8,128)(4,1)S(1)} %fusion.1, f32[128]{0:T(128)S(1)} %get-tuple-element.8, f32[128]{0:T(128)S(1)} %get-tuple-element.7, f32[128]{0:T(128)S(1)} %copy-done.3), kind=kOutput, calls=%fused_computation.8 | convolution fusion | flops 2148270080 | bytes 21628416 | tf_op jit(solution)/shard_map/dot_general | solution.py:48
  466.0 0.0 reduce-scatter.2.cloned.1.call-update
  466.0 2.3 convert_element_type.12
  468.3 0.1 dynamic_slice.9
  468.4 132.1 %reduce-scatter.2.cloned.1.call-done = f32[128,128]{1,0:T(8,128)} async-done(((f32[128,8192]{1,0:T(8,128)}), f32[128,128]{1,0:T(8,128)}) %reduce-scatter.2.cloned.1.call-update) | async-done | bytes 65552 | tf_op jit(solution)/shard_map/reduce_scatter | solution.py:54
  600.5 0.9 multiply_reduce_fusion.1
  601.5 129.2 %psum.23 = f32[128]{0:T(128)S(1)} all-reduce(f32[128]{0:T(128)S(1)} %multiply_reduce_fusion.1), channel_id=1, replica_groups=mesh['prompt'=4,'vocab'=64] {'vocab'}, use_global_device_ids=true, to_apply=%region_12.13 | all-reduce | flops 128 | bytes 1024 | tf_op jit(solution)/shard_map/psum | solution.py:56
  730.7 1.6 multiply_subtract_fusion
  (6 shorter events, 0.1 us)
Async XLA Ops:
  7.2 0.8 copy-start.2
  7.2 1.6 copy-start
  7.2 2.1 copy-start.1
  7.2 163.1 %all-gather.2.cloned.1.call-start = ((), (), s32[]{:S(2)}) async-start(), calls=%async_computation.1 | async-start | bytes 20971520 | tf_op jit(solution)/shard_map/all_gather | solution.py:19
  7.9 592.6 %reduce-scatter.2.cloned.1.call-start = ((), (), s32[]{:S(2)}) async-start(), calls=%async_computation.2 | async-start | bytes 4259840 | tf_op jit(solution)/shard_map/reduce_scatter | solution.py:54
  179.1 16.8 %copy-start.4 = (s32[128]{0:T(128)S(1)}, s32[128]{0:T(128)}, u32[]{:S(2)}) copy-start(s32[128]{0:T(128)} %param.10) | copy-start | bytes 1540
  179.1 273.4 %copy-start.3 = (f32[128]{0:T(128)S(1)}, f32[128]{0:T(128)}, u32[]{:S(2)}) copy-start(f32[128]{0:T(128)} %param.11) | copy-start | bytes 1540
Sparse Core Ops, SparseCore 0:
  9.8 160.4 all-gather.1
  466.1 134.3 reduce-scatter.1
where the time goes:
time: 739 us
  blocking collectives  382 us (52%)
  waiting for transfers between devices  292 us (40%)
  matrix products  22.3 us (3%)
  local copies, waits for them, and re-layouts  17.6 us (2%)
  between operations  14.2 us (2%)
  other arithmetic  10.9 us (1%)
    all_gather x1, waiting for transfers between devices, shards(): lax.all_gather(head, 'prompt', axis=0, tiled=True)  159 us
    reduce_scatter x1, waiting for transfers between devices, shards(): lax.psum_scatter(grad_full, 'vocab', scatter_dimension=1, tiled=True)  132 us
    psum x1, blocking collectives, shards(): row_term = lax.psum(jnp.sum(grad_cols * normed_cols, axis=1), 'vocab')  129 us
    psum x1, blocking collectives, shards(): sum_all, sum_ref = lax.psum((sum_all, sum_ref), 'vocab')  128 us
    pmax x1, blocking collectives, shards(): peak_all, peak_ref = lax.pmax((peak_all, peak_ref), 'vocab')  125 us
    gather x3, local copies, waits for them, and re-layouts, shards(): picked = jnp.take_along_axis(logits, safe_ids, axis=1)  16.8 us
  transfers between devices with their start and end apart: 2, of which 2 were waited for; matrix products, arithmetic and copies ran while one was open for 1% of the time, Pallas kernels for 0%

commit v1 on v0

--- a/solution.py
+++ b/solution.py
@@ -7,6 +7,28 @@
 lowest = -1e30
 
 
+def laid_out(blocks, dim):
+    blocks = jnp.moveaxis(blocks, 0, dim)
+    lengths = blocks.shape
+    return blocks.reshape(*lengths[:dim], lengths[dim] * lengths[dim + 1], *lengths[dim + 2 :])
+
+
+def collect(x, axis, dim):
+    count = lax.axis_size(axis)
+    pairs = [(i, (i + 1) % count) for i in range(count)]
+    back = [(b, a) for a, b in pairs]
+    lower, upper = ([], [])
+    for step in range(count - 1):
+        if step % 2 == 0:
+            lower.append(lax.ppermute(lower[-1] if lower else x, axis, pairs))
+        else:
+            upper.append(lax.ppermute(upper[-1] if upper else x, axis, back))
+    pieces = jnp.stack([*lower[::-1], x, *upper])
+    shift = lax.axis_index(axis) - len(lower)
+    pieces = pieces[(jnp.arange(count) - shift) % count]
+    return laid_out(pieces, dim)
+
+
 def shards(hidden, head, gain, refusal_ids, refusal_count, loss_scale):
     row_count, model_width = hidden.shape
     vocab_local = head.shape[1]
@@ -14,11 +36,7 @@
     hidden_f = hidden.astype(jnp.float32)
     inverse_rms = lax.rsqrt(jnp.mean(hidden_f * hidden_f, axis=1, keepdims=True) + epsilon)
     normed = (hidden_f * inverse_rms * gain).astype(jnp.bfloat16)
-    logits = jnp.dot(
-        normed,
-        lax.all_gather(head, "prompt", axis=0, tiled=True),
-        preferred_element_type=jnp.float32,
-    )
+    logits = jnp.dot(normed, collect(head, "prompt", 0), preferred_element_type=jnp.float32)
     vocab_start = lax.axis_index("vocab") * vocab_local
     shifted_ids = refusal_ids - vocab_start
     in_list = jnp.arange(list_length)[None, :] < refusal_count[:, None]

time: 739 us -> 933 us (1.26)
  waiting for transfers between devices: 292 us -> 437 us
  local copies, waits for them, and re-layouts: 17.6 us -> 40.6 us
  other arithmetic: 10.9 us -> 32.3 us
    ppermute x0 -> x3, waiting for transfers between devices: none -> 306 us  [the longest x2 306 us: collect(): lower.append(lax.ppermute(lower[-1] if lower else x, axis, pairs))]
    all_gather x1, waiting for transfers between devices: 159 us -> 0.02 us  [shards(): lax.all_gather(head, 'prompt', axis=0, tiled=True)]
    gather x0 -> x4, local copies, waits for them, and re-layouts: none -> 22.8 us  [collect(): pieces = pieces[(jnp.arange(count) - shift) % count]]
  transfers between devices with their start and end apart: 2 -> 5, of which waited for: 2 -> 3; matrix products, arithmetic and copies ran while one was open for 1% -> 8% of each run, Pallas kernels for 0% -> 0%
where the time goes in v1:
time: 933 us; the launch traced here: 932 us
  waiting for transfers between devices  437 us (47%)
  blocking collectives  386 us (41%)
  local copies, waits for them, and re-layouts  40.6 us (4%)
  other arithmetic  32.3 us (3%)
  matrix products  15.9 us (2%)
  between operations  14.2 us (2%)
    ppermute x2, waiting for transfers between devices, collect(): lower.append(lax.ppermute(lower[-1] if lower else x, axis, pairs))  306 us
    reduce_scatter x1, waiting for transfers between devices, shards(): lax.psum_scatter(grad_full, 'vocab', scatter_dimension=1, tiled=True)  130 us
    pmax x1, blocking collectives, shards(): peak_all, peak_ref = lax.pmax((peak_all, peak_ref), 'vocab')  130 us
    psum x1, blocking collectives, shards(): row_term = lax.psum(jnp.sum(grad_cols * normed_cols, axis=1), 'vocab')  129 us
    psum x1, blocking collectives, shards(): sum_all, sum_ref = lax.psum((sum_all, sum_ref), 'vocab')  127 us
    gather x4, local copies, waits for them, and re-layouts, collect(): pieces = pieces[(jnp.arange(count) - shift) % count]  22.8 us
  transfers between devices with their start and end apart: 5, of which 3 were waited for; matrix products, arithmetic and copies ran while one was open for 8% of the time, Pallas kernels for 0%

profile of v1, /device:TPU:1, one launch (start us, length us, event | category | flops | bytes accessed | tf_op | source)
XLA Modules:
  0.0 932.0 jit_solution(4105729861556939051)
XLA Ops:
  7.2 0.7 all-gather.2.cloned.1.call-update
  8.0 2.1 collective-permute-start
  10.1 1.4 collective-permute-start.2
  11.4 156.1 %collective-permute-done = bf16[2048,1024]{1,0:T(8,128)(2,1)} collective-permute-done((bf16[2048,1024]{1,0:T(8,128)(2,1)}, bf16[2048,1024]{1,0:T(8,128)(2,1)}, u32[]{:S(2)}, u32[]{:S(2)}) %collective-permute-start) | collective-permute-done | bytes 4194336 | tf_op jit(solution)/shard_map/ppermute | solution.py:23
  167.6 2.2 collective-permute-start.1
  169.8 0.8 copy.11
  170.6 0.1 reshape.92
  170.7 2.3 multiply_reduce_fusion
  173.0 1.9 multiply_convert_fusion
  174.9 150.4 %collective-permute-done.1 = bf16[2048,1024]{1,0:T(8,128)(2,1)} collective-permute-done((bf16[2048,1024]{1,0:T(8,128)(2,1)}, bf16[2048,1024]{1,0:T(8,128)(2,1)}, u32[]{:S(2)}, u32[]{:S(2)}) %collective-permute-start.1) | collective-permute-done | bytes 4194336 | tf_op jit(solution)/shard_map/ppermute | solution.py:23
  325.3 7.3 pad_maximum_fusion
  332.6 5.0 fusion.14
  337.7 6.4 gather_fusion.1
  344.0 6.4 gather_fusion.2
  350.4 3.6 pad_maximum_fusion.2
  354.1 5.0 gather_fusion.3
  359.1 8.7 pad_maximum_fusion.1
  367.8 2.5 fusion.15
  370.3 16.6 %gather_fusion = f32[2048]{0:T(1024)S(1)} fusion(f32[128,1024]{1,0:T(8,128)S(1)} %get-tuple-element.18, s32[2048]{0:T(1024)S(1)} %reshape.92), kind=kCustom, calls=%fused_computation | custom fusion | bytes 32768 | tf_op jit(solution)/shard_map/jit(take_along_axis)/gather | solution.py:45
  387.0 0.2 select_reduce_fusion
  387.2 129.6 %all-reduce.1 = (f32[128]{0:T(128)S(1)}, f32[128]{0:T(128)S(1)}) all-reduce(f32[128]{0:T(128)S(1)} %get-tuple-element.17, f32[128]{0:T(128)S(1)} %get-tuple-element.9), channel_id=1, replica_groups=mesh['prompt'=4,'vocab'=64] {'vocab'}, use_global_device_ids=true, to_apply=%region_7.8 | all-reduce | flops 256 | bytes 2048 | tf_op jit(solution)/shard_map/pmax | solution.py:48
  516.8 0.2 exponential_reduce_fusion.1
  517.0 0.2 exponential_reduce_fusion
  517.2 127.5 %all-reduce = (f32[128]{0:T(128)S(1)}, f32[128]{0:T(128)S(1)}) all-reduce(f32[128]{0:T(128)S(1)} %exponential_reduce_fusion, f32[128]{0:T(128)S(1)} %exponential_reduce_fusion.1), channel_id=1, replica_groups=mesh['prompt'=4,'vocab'=64] {'vocab'}, use_global_device_ids=true, to_apply=%region_9.10 | all-reduce | flops 256 | bytes 2048 | tf_op jit(solution)/shard_map/psum | solution.py:51
  644.7 0.5 fusion.12
  645.2 2.4 fusion.1
  647.6 13.5 %fusion.2 = f32[128,8192]{1,0:T(8,128)} fusion(bf16[8192,1024]{1,0:T(8,128)(2,1)} %all-gather.2.cloned.1.call-done, f32[128,1024]{1,0:T(8,128)S(1)} %get-tuple-element.18, pred[128,1024]{1,0:T(8,128)(4,1)S(1)} %fusion.1, f32[128]{0:T(128)S(1)} %get-tuple-element.8, f32[128]{0:T(128)S(1)} %get-tuple-element.7, f32[128]{0:T(128)S(1)} %copy-done.4), kind=kOutput, calls=%fused_computation.14 | convolution fusion | flops 2148270080 | bytes 21628416 | tf_op jit(solution)/shard_map/dot_general | solution.py:66
  661.1 2.3 convert_element_type.12
  663.5 129.8 %reduce-scatter.2.cloned.1.call-done = f32[128,128]{1,0:T(8,128)} async-done(((f32[128,8192]{1,0:T(8,128)}), f32[128,128]{1,0:T(8,128)}) %reduce-scatter.2.cloned.1.call-update) | async-done | bytes 65552 | tf_op jit(solution)/shard_map/reduce_scatter | solution.py:72
  793.4 0.9 multiply_reduce_fusion.1
  794.3 129.2 %psum.23 = f32[128]{0:T(128)S(1)} all-reduce(f32[128]{0:T(128)S(1)} %multiply_reduce_fusion.1), channel_id=1, replica_groups=mesh['prompt'=4,'vocab'=64] {'vocab'}, use_global_device_ids=true, to_apply=%region_12.13 | all-reduce | flops 128 | bytes 1024 | tf_op jit(solution)/shard_map/psum | solution.py:74
  923.5 1.6 multiply_subtract_fusion
  (23 shorter events, 0.4 us)
Async XLA Ops:
  7.2 165.9 %copy-start.1 = (bf16[128,8192]{1,0:T(8,128)(2,1)S(1)}, bf16[128,8192]{1,0:T(8,128)(2,1)}, u32[]{:S(2)}) copy-start(bf16[128,8192]{1,0:T(8,128)(2,1)} %param.6) | copy-start | bytes 6291460
  7.2 165.9 %copy-start.3 = (f32[8192]{0:T(1024)S(1)}, f32[8192]{0:T(1024)}, u32[]{:S(2)}) copy-start(f32[8192]{0:T(1024)} %param.8) | copy-start | bytes 98308
  7.2 640.4 %all-gather.2.cloned.1.call-start = ((), (), s32[]{:S(2)}) async-start(), calls=%async_computation.1 | async-start | bytes 20971520 | tf_op jit(solution)/shard_map/all_gather | solution.py:68
  7.9 785.4 %reduce-scatter.2.cloned.1.call-start = ((), (), s32[]{:S(2)}) async-start(), calls=%async_computation.2 | async-start | bytes 4259840 | tf_op jit(solution)/shard_map/reduce_scatter | solution.py:72
  8.0 159.6 %collective-permute-start = (bf16[2048,1024]{1,0:T(8,128)(2,1)}, bf16[2048,1024]{1,0:T(8,128)(2,1)}, u32[]{:S(2)}, u32[]{:S(2)}) collective-permute-start(bf16[2048,1024]{1,0:T(8,128)(2,1)} %param.7), channel_id=1, source_target_pairs={{0,64},{64,128},{128,192},{192,0},{1,65},{65,129},{129,193},{193,1... | collective-permute-start | bytes 12582920 | tf_op jit(solution)/shard_map/ppermute | solution.py:23
  10.1 164.9 %collective-permute-start.2 = (bf16[2048,1024]{1,0:T(8,128)(2,1)}, bf16[2048,1024]{1,0:T(8,128)(2,1)}, u32[]{:S(2)}, u32[]{:S(2)}) collective-permute-start(bf16[2048,1024]{1,0:T(8,128)(2,1)} %param.7), channel_id=1, source_target_pairs={{64,0},{128,64},{192,128},{0,192},{65,1},{129,65},{193,129},{1,193... | collective-permute-start | bytes 12582920 | tf_op jit(solution)/shard_map/ppermute | solution.py:25
  167.6 157.7 %collective-permute-start.1 = (bf16[2048,1024]{1,0:T(8,128)(2,1)}, bf16[2048,1024]{1,0:T(8,128)(2,1)}, u32[]{:S(2)}, u32[]{:S(2)}) collective-permute-start(bf16[2048,1024]{1,0:T(8,128)(2,1)} %collective-permute-done), channel_id=1, source_target_pairs={{0,64},{64,128},{128,192},{192,0},{1,65},{65,129},{129,193},{193,1... | collective-permute-start | bytes 12582920 | tf_op jit(solution)/shard_map/ppermute | solution.py:23
  170.7 154.6 %copy-start = (bf16[2048,1024]{1,0:T(8,128)(2,1)S(1)}, bf16[2048,1024]{1,0:T(8,128)(2,1)}, u32[]{:S(2)}) copy-start(bf16[2048,1024]{1,0:T(8,128)(2,1)} %param.7) | copy-start | bytes 12582916
  359.1 8.7 copy-start.2
  370.3 16.8 %copy-start.5 = (s32[128]{0:T(128)S(1)}, s32[128]{0:T(128)}, u32[]{:S(2)}) copy-start(s32[128]{0:T(128)} %param.10) | copy-start | bytes 1540
  370.3 277.4 %copy-start.4 = (f32[128]{0:T(128)S(1)}, f32[128]{0:T(128)}, u32[]{:S(2)}) copy-start(f32[128]{0:T(128)} %param.11) | copy-start | bytes 1540
Sparse Core Ops, SparseCore 0:
  9.8 290.0 all-gather.1
  661.2 132.0 reduce-scatter.1
